TPU v7x, 512 devices: a whole 4x8x8 slice. The times are simulated.
512 devices in a mesh: row: 16 (over z, y_lo), col: 32 (over x, y_hi, core).
Axes of the slice: x: 4, y: 8 (y_hi: 4, y_lo: 2; y = y_hi * 2 + y_lo), z: 8, core: 2. Of those that a mesh axis runs over, the one named last changes fastest.
Arguments:
- features: bfloat16 [65536, 128], P(('col', 'row')), may hold values from -6 to 6
- grad_out: bfloat16 [65536, 128], P(('row', 'col')), may hold values from -6 to 6
- weight: bfloat16 [128, 128], replicated, may hold values from -0.5 to 0.5
- block_ids: int32 [16, 32, 152], P('row', 'col'), may hold values from 0 to 511, as said below
- block_vals: bfloat16 [16, 32, 152, 128, 128], P('row', 'col'), may hold values from -0.0390625 to 0.0390625
- block_count: int32 [16, 32], P('row', 'col'), may hold values from 1 to 152
- node_perm: int32 [512, 128], P(('col', 'row')), may hold values from 0 to 127, each once within a row
Outputs:
- feature_grad: bfloat16 [65536, 128], P(('col', 'row'))
- weight_grad: float32 [128, 128], replicated
Inputs may be any that keep to these rules, and one draw needn't show every extreme that they name: `block_ids`: in each tile the 152 entries are distinct block positions p * 16 + q; slots at or beyond block_count are empty and must be ignored. `node_perm`: each row is a permutation of 0 to 127.
All inputs are finite; a program needn't handle non-finite values.
Results may differ from a plain program's by a relative error of at most 0.0059.
Values may be sent and summed in bfloat16 or wider, within the bound.
A program may use at most 128 MiB of HBM per device.

v0:
```python
import math
import jax
import jax.numpy as jnp
from jax import lax
from jax.sharding import PartitionSpec as P

BLOCK = 128


def grad_step(agg_low, grad_rows, weight):
    pre = jnp.dot(agg_low, weight, preferred_element_type=jnp.float32)
    sigma = jax.nn.sigmoid(pre)
    grad_pre = (grad_rows.astype(jnp.float32) * sigma * (1.0 + pre * (1.0 - sigma))).astype(
        jnp.bfloat16
    )
    grad_agg = lax.dot_general(
        grad_pre, weight, (((1,), (1,)), ((), ())), preferred_element_type=jnp.float32
    )
    return (grad_pre, grad_agg.astype(jnp.bfloat16))


def block_sums(product, targets, live, segments):
    routed = jnp.where(live, targets, segments)
    summed = jax.ops.segment_sum(product, routed, num_segments=segments + 1)
    return summed[:segments]


def shards(features, grad_out, weight, block_ids, block_vals, block_count, node_perm):
    nodes_dev = grad_out.shape[0]
    hidden = weight.shape[0]
    tile_ids = block_ids[0, 0]
    values = block_vals[0, 0]
    count_live = block_count[0, 0]
    slots_tile = tile_ids.shape[0]
    row_count = nodes_dev * lax.axis_size("col") // BLOCK
    col_count = nodes_dev * lax.axis_size("row") // BLOCK
    total_nodes = nodes_dev * lax.axis_size("row") * lax.axis_size("col")
    live = jnp.arange(slots_tile, dtype=jnp.int32) < count_live
    block_row = tile_ids // col_count
    block_col = tile_ids % col_count
    column_source = lax.all_gather(features, "row", axis=0, tiled=True)
    picked = column_source.reshape(col_count, BLOCK, hidden)[block_col]
    product = jnp.einsum("kij,kjf->kif", values, picked, preferred_element_type=jnp.float32)
    partial_value = block_sums(product, block_row, live, row_count).reshape(
        row_count * BLOCK, hidden
    )
    aggregate = lax.psum_scatter(partial_value, "col", scatter_dimension=0, tiled=True)
    agg_low = aggregate.astype(jnp.bfloat16)
    grad_pre, grad_share = grad_step(agg_low, grad_out, weight)
    weight_part = jnp.dot(agg_low.T, grad_pre, preferred_element_type=jnp.float32)
    grad_rows = lax.all_gather(grad_share, "col", axis=0, tiled=True)
    weight_grad = lax.psum(weight_part, ("row", "col")) * (1.0 / math.sqrt(total_nodes))
    picked_back = grad_rows.reshape(row_count, BLOCK, hidden)[block_row]
    product_back = jnp.einsum(
        "kij,kif->kjf", values, picked_back, preferred_element_type=jnp.float32
    )
    partial_back = block_sums(product_back, block_col, live, col_count).reshape(
        col_count * BLOCK, hidden
    )
    grad_share_cols = lax.psum_scatter(partial_back, "row", scatter_dimension=0, tiled=True)
    rounded = grad_share_cols.astype(jnp.bfloat16)
    feature_grad = rounded[node_perm[0]]
    return (feature_grad, weight_grad)


def solution(mesh):
    in_specs = (
        P(("col", "row"), None),
        P(("row", "col"), None),
        P(),
        P("row", "col", None),
        P("row", "col", None, None, None),
        P("row", "col"),
        P(("col", "row"), None),
    )
    out_specs = (P(("col", "row"), None), P())
    return jax.shard_map(shards, mesh=mesh, in_specs=in_specs, out_specs=out_specs, check_vma=False)
```

profile of v0, /device:TPU:4, one launch (start us, length us, event | category | flops | bytes accessed | tf_op | source)
XLA Modules:
  0.0 607.2 jit_solution(2033896433721760579)
XLA Ops:
  7.2 0.0 reduce-scatter.3.cloned.1.call-start
  7.2 0.7 compare_select_fusion
  8.6 44.5 %all_gather.6 = bf16[2048,128]{1,0:T(8,128)(2,1)S(1)} all-gather(bf16[128,128]{1,0:T(8,128)(2,1)} %param.7), channel_id=1, replica_groups=mesh['row'=16,'col'=32] {'row'}, dimensions={0}, use_global_device_ids=true | all-gather | bytes 557056 | tf_op jit(solution)/shard_map/all_gather | solution.py:41
  53.1 7.7 %gather_fusion = bf16[152,128,128]{2,1,0:T(8,128)(2,1)} fusion(bf16[16,128,128]{2,1,0:T(8,128)(2,1)S(1)} %bitcast.46, s32[1024]{0:T(1024)S(1)} %pad_clamp_fusion.2), kind=kCustom, calls=%fused_computation | custom fusion | bytes 9962080 | tf_op jit(solution)/shard_map/gather | solution.py:42
  60.8 11.3 %fusion.4 = f32[152,128,128]{1,2,0:T(8,128)} fusion(bf16[152,128,128]{2,1,0:T(8,128)(2,1)} %gather_fusion, bf16[1,1,152,128,128]{4,3,2,1,0:T(8,128)(2,1)} %param.11), kind=kOutput, calls=%fused_computation.9 | convolution fusion | flops 637534208 | bytes 19922944 | tf_op jit(solution)/shard_map/kij,kjf->kif/dot_general | solution.py:43
  72.1 11.3 %copy.12 = f32[152,128,128]{2,1,0:T(8,128)} copy(f32[152,128,128]{1,2,0:T(8,128)} %fusion.4) | data formatting | bytes 19922944 | tf_op jit(solution)/shard_map/kij,kjf->kif/dot_general | solution.py:43
  83.5 0.2 broadcast_in_dim.17
  83.7 21.0 %scatter_fusion = f32[33,128,128]{2,1,0:T(8,128)S(1)} fusion(f32[33,128,128]{2,1,0:T(8,128)S(1)} %broadcast_in_dim.17, s32[152]{0:T(256)S(1)} %bitcast.51, f32[152,128,128]{2,1,0:T(8,128)} %copy.12), kind=kCustom, calls=%fused_computation.3 | custom fusion | flops 2490368 | bytes 29885024 | tf_op jit(solution)/shard_map/scatter-add | solution.py:24
  104.7 1.5 slice.14
  106.2 0.0 reduce-scatter.3.cloned.1.call-update
  106.2 0.0 all-gather.2.cloned.1.call-start
  106.2 94.5 %reduce-scatter.3.cloned.1.call-done = f32[128,128]{1,0:T(8,128)} async-done(((f32[4096,128]{1,0:T(8,128)}), f32[128,128]{1,0:T(8,128)}) %reduce-scatter.3.cloned.1.call-update) | async-done | bytes 65552 | tf_op jit(solution)/shard_map/reduce_scatter | solution.py:47
  200.8 1.0 multiply_convert_fusion
  201.8 0.8 convolution_convert_fusion
  202.5 0.0 all-gather.2.cloned.1.call-update
  202.6 0.0 all-reduce.2.cloned.1.call-start
  202.6 1.7 fusion.10
  204.3 0.0 all-reduce.2.cloned.1.call-update
  204.3 0.2 reduce-scatter.5.cloned.1.call-start
  204.5 54.7 %all-gather.2.cloned.1.call-done = bf16[4096,128]{1,0:T(8,128)(2,1)} async-done(((bf16[128,128]{1,0:T(8,128)(2,1)}), bf16[4096,128]{1,0:T(8,128)(2,1)}) %all-gather.2.cloned.1.call-update) | async-done | bytes 1048592 | tf_op jit(solution)/shard_map/all_gather | solution.py:51
  259.3 8.9 %gather_fusion.1 = bf16[152,128,128]{2,1,0:T(8,128)(2,1)} fusion(bf16[32,128,128]{2,1,0:T(8,128)(2,1)} %bitcast.47, s32[1024]{0:T(1024)S(1)} %pad_clamp_fusion.1), kind=kCustom, calls=%fused_computation.1 | custom fusion | bytes 9962080 | tf_op jit(solution)/shard_map/gather | solution.py:53
  268.2 9.5 %fusion.7 = f32[152,128,128]{1,2,0:T(8,128)} fusion(bf16[152,128,128]{2,1,0:T(8,128)(2,1)} %gather_fusion.1, bf16[1,1,152,128,128]{4,3,2,1,0:T(8,128)(2,1)} %param.11), kind=kOutput, calls=%fused_computation.10 | convolution fusion | flops 637534208 | bytes 19922944 | tf_op jit(solution)/shard_map/kij,kif->kjf/dot_general | solution.py:54
  277.7 11.3 %copy.14 = f32[152,128,128]{2,1,0:T(8,128)} copy(f32[152,128,128]{1,2,0:T(8,128)} %fusion.7) | data formatting | bytes 19922944 | tf_op jit(solution)/shard_map/kij,kif->kjf/dot_general | solution.py:54
  289.0 0.1 broadcast_in_dim.16
  289.2 21.0 %scatter_fusion.1 = f32[17,128,128]{2,1,0:T(8,128)S(1)} fusion(f32[17,128,128]{2,1,0:T(8,128)S(1)} %broadcast_in_dim.16, s32[152]{0:T(256)S(1)} %bitcast.50, f32[152,128,128]{2,1,0:T(8,128)} %copy.14), kind=kCustom, calls=%fused_computation.4 | custom fusion | flops 2490368 | bytes 29885024 | tf_op jit(solution)/shard_map/scatter-add | solution.py:24
  310.1 1.0 slice.15
  311.2 0.0 reduce-scatter.5.cloned.1.call-update
  311.2 211.2 %all-reduce.2.cloned.1.call-done = f32[128,128]{1,0:T(8,128)} async-done(((f32[128,128]{1,0:T(8,128)}), f32[128,128]{1,0:T(8,128)}) %all-reduce.2.cloned.1.call-update) | async-done | bytes 65552 | tf_op jit(solution)/shard_map/psum | solution.py:52
  522.4 1.5 broadcast_multiply_fusion
  523.9 74.6 %reduce-scatter.5.cloned.1.call-done = f32[128,128]{1,0:T(8,128)} async-done(((f32[2048,128]{1,0:T(8,128)}), f32[128,128]{1,0:T(8,128)}) %reduce-scatter.5.cloned.1.call-update) | async-done | bytes 65552 | tf_op jit(solution)/shard_map/reduce_scatter | solution.py:60
  598.5 0.8 convert_element_type.19
  599.4 1.3 gather_fusion.2
  (11 shorter events, 0.1 us)
Async XLA Ops:
  7.2 193.6 %copy-start = (bf16[128,128]{1,0:T(8,128)(2,1)S(1)}, bf16[128,128]{1,0:T(8,128)(2,1)}, u32[]{:S(2)}) copy-start(bf16[128,128]{1,0:T(8,128)(2,1)} %param.9) | copy-start | bytes 98308
  7.2 193.6 %reduce-scatter.3.cloned.1.call-start = ((), (), s32[]{:S(2)}) async-start(), calls=%async_computation.2 | async-start | bytes 2162688 | tf_op jit(solution)/shard_map/reduce_scatter | solution.py:47
  104.7 96.1 %copy-start.1 = (bf16[128,128]{1,0:T(8,128)(2,1)S(1)}, bf16[128,128]{1,0:T(8,128)(2,1)}, u32[]{:S(2)}) copy-start(bf16[128,128]{1,0:T(8,128)(2,1)} %param.8) | copy-start | bytes 98308
  106.2 153.1 %all-gather.2.cloned.1.call-start = ((), (), s32[]{:S(2)}) async-start(), calls=%async_computation.3 | async-start | bytes 1081344 | tf_op jit(solution)/shard_map/all_gather | solution.py:51
  202.6 319.9 %all-reduce.2.cloned.1.call-start = ((), (), s32[]{:S(2)}) async-start(), calls=%async_computation.5 | async-start | bytes 131072 | tf_op jit(solution)/shard_map/psum | solution.py:52
  204.3 394.2 %reduce-scatter.5.cloned.1.call-start = ((), (), s32[]{:S(2)}) async-start(), calls=%async_computation.4 | async-start | bytes 1114112 | tf_op jit(solution)/shard_map/reduce_scatter | solution.py:60
  289.2 22.1 %copy-start.2 = (s32[1,128]{1,0:T(1,128)S(1)}, s32[1,128]{1,0:T(1,128)}, u32[]{:S(2)}) copy-start(s32[1,128]{1,0:T(1,128)} %param.13) | copy-start | bytes 1540
Sparse Core Ops, SparseCore 0:
  106.3 94.3 reduce-scatter.2
  204.5 54.7 all-gather.1
  264.8 257.5 all-reduce.1
  525.1 73.4 reduce-scatter.4
where the time goes:
time: 609 us; the launch traced here: 607 us
  waiting for transfers between devices  435 us (71%)
  other arithmetic  45 us (7%)
  blocking collectives  44.5 us (7%)
  local copies, waits for them, and re-layouts  43.5 us (7%)
  matrix products  24.3 us (4%)
  between operations  14.5 us (2%)
    psum x1, waiting for transfers between devices, shards(): lax.psum(weight_part, ('row', 'col')) * (1.0 / math.sqrt(total_nodes))  211 us
    reduce_scatter x1, waiting for transfers between devices, shards(): lax.psum_scatter(partial_value, 'col', scatter_dimension=0, tiled=True)  94.5 us
    reduce_scatter x1, waiting for transfers between devices, shards(): lax.psum_scatter(partial_back, 'row', scatter_dimension=0, tiled=True)  74.6 us
    all_gather x1, waiting for transfers between devices, shards(): grad_rows = lax.all_gather(grad_share, 'col', axis=0, tiled=True)  54.7 us
    all_gather x1, blocking collectives, shards(): column_source = lax.all_gather(features, 'row', axis=0, tiled=True)  44.5 us
    scatter-add x2, other arithmetic, block_sums(): summed = jax.ops.segment_sum(product, routed, num_segments=segments + 1)  41.9 us
  transfers between devices with their start and end apart: 4, of which 4 were waited for; matrix products, arithmetic and copies ran while one was open for 9% of the time, Pallas kernels for 0%

commit v1 on v0

--- a/solution.py
+++ b/solution.py
@@ -1,3 +1,4 @@
+import functools
 import math
 import jax
 import jax.numpy as jnp
@@ -5,6 +6,18 @@
 from jax.sharding import PartitionSpec as P
 
 BLOCK = 128
+
+
+def _assign_skins(piece_in, axis_tag):
+    runs = []
+    for _ in range(lax.axis_size(axis_tag)):
+        runs.append(piece_in)
+    kept_arr = jnp.stack(runs, axis=0)
+    taken_in = lax.all_to_all(kept_arr, axis_tag, 0, 0)
+    return jnp.concatenate(taken_in, axis=0)
+
+
+guide_desk = functools.partial(_assign_skins, axis_tag="col")
 
 
 def grad_step(agg_low, grad_rows, weight):
@@ -48,7 +61,7 @@
     agg_low = aggregate.astype(jnp.bfloat16)
     grad_pre, grad_share = grad_step(agg_low, grad_out, weight)
     weight_part = jnp.dot(agg_low.T, grad_pre, preferred_element_type=jnp.float32)
-    grad_rows = lax.all_gather(grad_share, "col", axis=0, tiled=True)
+    grad_rows = guide_desk(grad_share)
     weight_grad = lax.psum(weight_part, ("row", "col")) * (1.0 / math.sqrt(total_nodes))
     picked_back = grad_rows.reshape(row_count, BLOCK, hidden)[block_row]
     product_back = jnp.einsum(

time: 609 us -> 563 us (0.924)
  waiting for transfers between devices: 435 us -> 383 us
  starting transfers between devices: 0.34 us -> 7.68 us
    all_gather x1 -> x0, waiting for transfers between devices: 54.7 us -> none  [shards(): grad_rows = lax.all_gather(grad_share, 'col', axis=0, tiled=True)]
    all_to_all x0 -> x1, waiting for transfers between devices: none -> 25.6 us  [_assign_skins(): taken_in = lax.all_to_all(kept_arr, axis_tag, 0, 0)]
    psum x1, waiting for transfers between devices: 211 us -> 188 us  [shards(): lax.psum(weight_part, ('row', 'col')) * (1.0 / math.sqrt(total_nodes))]
    all_to_all x0 -> x1, starting transfers between devices: none -> 7.38 us  [_assign_skins(): taken_in = lax.all_to_all(kept_arr, axis_tag, 0, 0)]
  transfers between devices with their start and end apart: 4 -> 4, of which waited for: 4 -> 4; matrix products, arithmetic and copies ran while one was open for 9% -> 10% of each run, Pallas kernels for 0% -> 0%
where the time goes in v1:
time: 563 us; the launch traced here: 562 us
  waiting for transfers between devices  383 us (68%)
  other arithmetic  45 us (8%)
  blocking collectives  44.5 us (8%)
  local copies, waits for them, and re-layouts  43.4 us (8%)
  matrix products  23.7 us (4%)
  between operations  14.5 us (3%)
  starting transfers between devices  7.68 us (1%)
    psum x1, waiting for transfers between devices, shards(): lax.psum(weight_part, ('row', 'col')) * (1.0 / math.sqrt(total_nodes))  188 us
    reduce_scatter x1, waiting for transfers between devices, shards(): lax.psum_scatter(partial_value, 'col', scatter_dimension=0, tiled=True)  94.6 us
    reduce_scatter x1, waiting for transfers between devices, shards(): lax.psum_scatter(partial_back, 'row', scatter_dimension=0, tiled=True)  74.8 us
    all_gather x1, blocking collectives, shards(): column_source = lax.all_gather(features, 'row', axis=0, tiled=True)  44.5 us
    scatter-add x2, other arithmetic, block_sums(): summed = jax.ops.segment_sum(product, routed, num_segments=segments + 1)  41.9 us
    all_to_all x1, waiting for transfers between devices, _assign_skins(): taken_in = lax.all_to_all(kept_arr, axis_tag, 0, 0)  25.6 us
    dot_general x1, matrix products, shards(): jnp.einsum('kij,kjf->kif', values, picked, preferred_element_type=jnp.flo...  11.3 us
    dot_general x1, local copies, waits for them, and re-layouts, shards(): jnp.einsum('kij,kjf->kif', values, picked, preferred_element_type=jnp.flo...  11.3 us
  transfers between devices with their start and end apart: 4, of which 4 were waited for; matrix products, arithmetic and copies ran while one was open for 10% of the time, Pallas kernels for 0%

profile of v1, /device:TPU:4, one launch (start us, length us, event | category | flops | bytes accessed | tf_op | source)
XLA Modules:
  0.0 561.6 jit_solution(16592991521733176024)
XLA Ops:
  7.2 0.0 reduce-scatter.3.cloned.1.call-start
  7.2 0.7 compare_select_fusion
  8.6 44.5 %all_gather.3 = bf16[2048,128]{1,0:T(8,128)(2,1)S(1)} all-gather(bf16[128,128]{1,0:T(8,128)(2,1)} %param.7), channel_id=1, replica_groups=mesh['row'=16,'col'=32] {'row'}, dimensions={0}, use_global_device_ids=true | all-gather | bytes 557056 | tf_op jit(solution)/shard_map/all_gather | solution.py:54
  53.1 7.7 %gather_fusion = bf16[152,128,128]{2,1,0:T(8,128)(2,1)} fusion(bf16[16,128,128]{2,1,0:T(8,128)(2,1)S(1)} %bitcast.45, s32[1024]{0:T(1024)S(1)} %pad_clamp_fusion.2), kind=kCustom, calls=%fused_computation | custom fusion | bytes 9962080 | tf_op jit(solution)/shard_map/gather | solution.py:55
  60.8 11.3 %fusion.4 = f32[152,128,128]{1,2,0:T(8,128)} fusion(bf16[152,128,128]{2,1,0:T(8,128)(2,1)} %gather_fusion, bf16[1,1,152,128,128]{4,3,2,1,0:T(8,128)(2,1)} %param.11), kind=kOutput, calls=%fused_computation.9 | convolution fusion | flops 637534208 | bytes 19922944 | tf_op jit(solution)/shard_map/kij,kjf->kif/dot_general | solution.py:56
  72.1 11.3 %copy.12 = f32[152,128,128]{2,1,0:T(8,128)} copy(f32[152,128,128]{1,2,0:T(8,128)} %fusion.4) | data formatting | bytes 19922944 | tf_op jit(solution)/shard_map/kij,kjf->kif/dot_general | solution.py:56
  83.4 0.2 broadcast_in_dim.17
  83.7 21.0 %scatter_fusion = f32[33,128,128]{2,1,0:T(8,128)S(1)} fusion(f32[33,128,128]{2,1,0:T(8,128)S(1)} %broadcast_in_dim.17, s32[152]{0:T(256)S(1)} %bitcast.49, f32[152,128,128]{2,1,0:T(8,128)} %copy.12), kind=kCustom, calls=%fused_computation.3 | custom fusion | flops 2490368 | bytes 29885024 | tf_op jit(solution)/shard_map/scatter-add | solution.py:37
  104.7 1.5 slice.14
  106.2 0.0 reduce-scatter.3.cloned.1.call-update
  106.2 94.6 %reduce-scatter.3.cloned.1.call-done = f32[128,128]{1,0:T(8,128)} async-done(((f32[4096,128]{1,0:T(8,128)}), f32[128,128]{1,0:T(8,128)}) %reduce-scatter.3.cloned.1.call-update) | async-done | bytes 65552 | tf_op jit(solution)/shard_map/reduce_scatter | solution.py:60
  200.7 1.0 multiply_convert_fusion
  201.8 0.1 convolution_convert_fusion
  201.9 1.2 stack.2
  203.1 7.4 %all-to-all-start = ((bf16[32,128,128]{2,1,0:T(8,128)(2,1)}), bf16[32,128,128]{2,1,0:T(8,128)(2,1)S(1)}, u32[]{:S(2)}, u32[]{:S(2)}) async-start(bf16[32,128,128]{2,1,0:T(8,128)(2,1)} %stack.2), calls=%async_computation.1 | async-start | bytes 2097152 | tf_op jit(solution)/shard_map/all_to_all | solution.py:16
  210.5 0.0 all-reduce.2.cloned.1.call-start
  210.6 1.7 fusion.10
  212.2 0.0 all-reduce.2.cloned.1.call-update
  212.3 0.2 reduce-scatter.5.cloned.1.call-start
  212.5 25.6 %all-to-all-done = bf16[32,128,128]{2,1,0:T(8,128)(2,1)S(1)} async-done(((bf16[32,128,128]{2,1,0:T(8,128)(2,1)}), bf16[32,128,128]{2,1,0:T(8,128)(2,1)S(1)}, u32[]{:S(2)}, u32[]{:S(2)}) %all-to-all-start) | async-done | bytes 1048608 | tf_op jit(solution)/shard_map/all_to_all | solution.py:16
  238.1 7.7 %gather_fusion.1 = bf16[152,128,128]{2,1,0:T(8,128)(2,1)} fusion(bf16[32,128,128]{2,1,0:T(8,128)(2,1)S(1)} %all-to-all-done, s32[1024]{0:T(1024)S(1)} %pad_clamp_fusion.1), kind=kCustom, calls=%fused_computation.1 | custom fusion | bytes 9962080 | tf_op jit(solution)/shard_map/gather | solution.py:66
  245.8 9.5 %fusion.7 = f32[152,128,128]{1,2,0:T(8,128)} fusion(bf16[152,128,128]{2,1,0:T(8,128)(2,1)} %gather_fusion.1, bf16[1,1,152,128,128]{4,3,2,1,0:T(8,128)(2,1)} %param.11), kind=kOutput, calls=%fused_computation.10 | convolution fusion | flops 637534208 | bytes 19922944 | tf_op jit(solution)/shard_map/kij,kif->kjf/dot_general | solution.py:67
  255.3 11.3 %copy.14 = f32[152,128,128]{2,1,0:T(8,128)} copy(f32[152,128,128]{1,2,0:T(8,128)} %fusion.7) | data formatting | bytes 19922944 | tf_op jit(solution)/shard_map/kij,kif->kjf/dot_general | solution.py:67
  266.7 0.1 broadcast_in_dim.16
  266.8 21.0 %scatter_fusion.1 = f32[17,128,128]{2,1,0:T(8,128)S(1)} fusion(f32[17,128,128]{2,1,0:T(8,128)S(1)} %broadcast_in_dim.16, s32[152]{0:T(256)S(1)} %bitcast.48, f32[152,128,128]{2,1,0:T(8,128)} %copy.14), kind=kCustom, calls=%fused_computation.4 | custom fusion | flops 2490368 | bytes 29885024 | tf_op jit(solution)/shard_map/scatter-add | solution.py:37
  287.8 1.0 slice.15
  288.8 0.0 reduce-scatter.5.cloned.1.call-update
  288.9 187.8 %all-reduce.2.cloned.1.call-done = f32[128,128]{1,0:T(8,128)} async-done(((f32[128,128]{1,0:T(8,128)}), f32[128,128]{1,0:T(8,128)}) %all-reduce.2.cloned.1.call-update) | async-done | bytes 65552 | tf_op jit(solution)/shard_map/psum | solution.py:65
  476.6 1.5 broadcast_multiply_fusion
  478.1 74.8 %reduce-scatter.5.cloned.1.call-done = f32[128,128]{1,0:T(8,128)} async-done(((f32[2048,128]{1,0:T(8,128)}), f32[128,128]{1,0:T(8,128)}) %reduce-scatter.5.cloned.1.call-update) | async-done | bytes 65552 | tf_op jit(solution)/shard_map/reduce_scatter | solution.py:73
  552.9 0.8 convert_element_type.19
  553.7 1.3 gather_fusion.2
  (11 shorter events, 0.1 us)
Async XLA Ops:
  7.2 193.6 %copy-start = (bf16[128,128]{1,0:T(8,128)(2,1)S(1)}, bf16[128,128]{1,0:T(8,128)(2,1)}, u32[]{:S(2)}) copy-start(bf16[128,128]{1,0:T(8,128)(2,1)} %param.9) | copy-start | bytes 98308
  7.2 193.6 %reduce-scatter.3.cloned.1.call-start = ((), (), s32[]{:S(2)}) async-start(), calls=%async_computation.3 | async-start | bytes 2162688 | tf_op jit(solution)/shard_map/reduce_scatter | solution.py:60
  104.7 96.1 %copy-start.1 = (bf16[128,128]{1,0:T(8,128)(2,1)S(1)}, bf16[128,128]{1,0:T(8,128)(2,1)}, u32[]{:S(2)}) copy-start(bf16[128,128]{1,0:T(8,128)(2,1)} %param.8) | copy-start | bytes 98308
  203.1 35.0 %all-to-all-start = ((bf16[32,128,128]{2,1,0:T(8,128)(2,1)}), bf16[32,128,128]{2,1,0:T(8,128)(2,1)S(1)}, u32[]{:S(2)}, u32[]{:S(2)}) async-start(bf16[32,128,128]{2,1,0:T(8,128)(2,1)} %stack.2), calls=%async_computation.1 | async-start | bytes 2097152 | tf_op jit(solution)/shard_map/all_to_all | solution.py:16
  210.5 266.1 %all-reduce.2.cloned.1.call-start = ((), (), s32[]{:S(2)}) async-start(), calls=%async_computation.5 | async-start | bytes 131072 | tf_op jit(solution)/shard_map/psum | solution.py:65
  212.3 340.6 %reduce-scatter.5.cloned.1.call-start = ((), (), s32[]{:S(2)}) async-start(), calls=%async_computation.4 | async-start | bytes 1114112 | tf_op jit(solution)/shard_map/reduce_scatter | solution.py:73
  266.8 22.1 %copy-start.2 = (s32[1,128]{1,0:T(1,128)S(1)}, s32[1,128]{1,0:T(1,128)}, u32[]{:S(2)}) copy-start(s32[1,128]{1,0:T(1,128)} %param.13) | copy-start | bytes 1540
Sparse Core Ops, SparseCore 0:
  106.3 94.3 reduce-scatter.2
  216.9 259.6 all-reduce.1
  479.4 73.4 reduce-scatter.4
